TPU v7x, 32 devices: a whole 2x2x4 slice. The times are simulated.
32 devices in a mesh: orbit: 8 (over y, x, core), tile: 4 (over z).
Axes of the slice: x: 2, y: 2, z: 4, core: 2. Of those that a mesh axis runs over, the one named last changes fastest.
Arguments:
- tokens: bfloat16 [32, 256, 1280], P('orbit', 'tile'), may hold values from -6 to 6
- cotangent: bfloat16 [32, 256, 1280], P('orbit', 'tile'), may hold values from -60 to 60
- w_query: bfloat16 [1280, 1280], replicated, may hold values from -0.15625 to 0.15625
- w_key: bfloat16 [1280, 1280], replicated, may hold values from -0.15625 to 0.15625
- w_value: bfloat16 [1280, 1280], replicated, may hold values from -0.15625 to 0.15625
- conv_taps: float32 [3, 1280], replicated, may hold values from 0.3 to 1
- conv_bias: float32 [1280], replicated, may hold values from -2 to 2
Outputs:
- grad_tokens: bfloat16 [32, 256, 1280], P('orbit', 'tile')
All inputs are finite; a program needn't handle non-finite values.
Results may differ from a plain program's by a relative error of at most 0.009.
The roundings to bfloat16 on the way count: a program that leaves them out, or rounds other values in their place, can miss the bound.
Values may be sent and summed in bfloat16 or wider, within the bound.
No kernel may reach another device: no remote copies, remote signals or barrier semaphores. Data moves between devices by JAX's collectives and lax.ppermute only.
A program may use at most 64 MiB of HBM per device.

v0:
```python
import math
import jax
import jax.numpy as jnp
from jax import lax
from jax.sharding import PartitionSpec as P

HEAD_DIM = 64


def mix_whole(tokens, conv_taps, conv_bias):
    source = tokens.astype(jnp.float32)
    mixed = (
        conv_taps[0] * jnp.roll(source, 1, axis=0)
        + conv_taps[1] * source
        + conv_taps[2] * jnp.roll(source, -1, axis=0)
    )
    return (source + mixed + conv_bias).astype(jnp.bfloat16)


def unmix_whole(grad_hidden, conv_taps):
    source = grad_hidden.astype(jnp.float32)
    result = (
        source
        + conv_taps[0] * jnp.roll(source, -1, axis=0)
        + conv_taps[1] * source
        + conv_taps[2] * jnp.roll(source, 1, axis=0)
    )
    return result.astype(jnp.bfloat16)


def project_all(hidden, weights):
    flat_rows = hidden.reshape(-1, hidden.shape[-1])
    return tuple(
        (
            jnp.dot(flat_rows, weight, preferred_element_type=jnp.float32)
            .astype(jnp.bfloat16)
            .reshape(hidden.shape)
            for weight in weights
        )
    )


def back_project(grad_query, grad_key, grad_value, weights):
    full_shape = grad_query.shape
    channels = full_shape[-1]
    total = jnp.dot(
        grad_query.reshape(-1, channels), weights[0].T, preferred_element_type=jnp.float32
    )
    total = total + jnp.dot(
        grad_key.reshape(-1, channels), weights[1].T, preferred_element_type=jnp.float32
    )
    total = total + jnp.dot(
        grad_value.reshape(-1, channels), weights[2].T, preferred_element_type=jnp.float32
    )
    return total.astype(jnp.bfloat16).reshape(full_shape)


def attention_grads(query_rows, key_rows, value_rows, grad_rows):
    frames, tok_count, channels = query_rows.shape
    head_count = channels // HEAD_DIM
    inv_root = 1.0 / math.sqrt(HEAD_DIM)
    shape_heads = (frames, tok_count, head_count, HEAD_DIM)
    q_heads = query_rows.reshape(shape_heads)
    k_heads = key_rows.reshape(shape_heads)
    v_heads = value_rows.reshape(shape_heads)
    g_heads = grad_rows.reshape(shape_heads)
    scores = (
        jnp.einsum("fshd,gshd->shfg", q_heads, k_heads, preferred_element_type=jnp.float32)
        * inv_root
    )
    peak = jnp.max(scores, axis=-1, keepdims=True)
    expo_terms = jnp.exp(scores - peak)
    attn_prob = expo_terms / jnp.sum(expo_terms, axis=-1, keepdims=True)
    prob_low = attn_prob.astype(jnp.bfloat16)
    attn_out = jnp.einsum("shfg,gshd->fshd", prob_low, v_heads, preferred_element_type=jnp.float32)
    row_delta = jnp.sum(g_heads.astype(jnp.float32) * attn_out, axis=-1)
    grad_value = jnp.einsum(
        "shfg,fshd->gshd", prob_low, g_heads, preferred_element_type=jnp.float32
    ).astype(jnp.bfloat16)
    grad_prob = jnp.einsum("fshd,gshd->shfg", g_heads, v_heads, preferred_element_type=jnp.float32)
    d_scores = attn_prob * (grad_prob - jnp.transpose(row_delta, (1, 2, 0))[..., None])
    scores_low = d_scores.astype(jnp.bfloat16)
    grad_query = (
        jnp.einsum("shfg,gshd->fshd", scores_low, k_heads, preferred_element_type=jnp.float32)
        * inv_root
    ).astype(jnp.bfloat16)
    grad_key = (
        jnp.einsum("shfg,fshd->gshd", scores_low, q_heads, preferred_element_type=jnp.float32)
        * inv_root
    ).astype(jnp.bfloat16)
    full_shape = (frames, tok_count, channels)
    return (
        grad_query.reshape(full_shape),
        grad_key.reshape(full_shape),
        grad_value.reshape(full_shape),
    )


def shards(tokens, cotangent, w_query, w_key, w_value, conv_taps, conv_bias):
    frame_rows, tile_rows, channels = tokens.shape
    spatial_all = tile_rows * lax.axis_size("tile")
    grad_f = cotangent.astype(jnp.float32)
    energy = lax.psum(jnp.sum(grad_f * grad_f, axis=(1, 2)), "tile")
    factor = lax.rsqrt(energy / (spatial_all * channels) + 1e-06)
    grad_out = (grad_f * factor[:, None, None]).astype(jnp.bfloat16)
    weights = (w_query, w_key, w_value)
    tokens_all, grad_all = (
        lax.all_to_all(tokens, "orbit", split_axis=1, concat_axis=0, tiled=True),
        lax.all_to_all(grad_out, "orbit", split_axis=1, concat_axis=0, tiled=True),
    )
    hidden_all = mix_whole(tokens_all, conv_taps, conv_bias)
    query_all, key_all, value_all = project_all(hidden_all, weights)
    grad_query, grad_key, grad_value = attention_grads(query_all, key_all, value_all, grad_all)
    grad_hidden = back_project(grad_query, grad_key, grad_value, weights)
    grad_input = unmix_whole(grad_hidden, conv_taps)
    return lax.all_to_all(grad_input, "orbit", split_axis=0, concat_axis=1, tiled=True)


def solution(mesh):
    in_specs = (P("orbit", "tile", None), P("orbit", "tile", None), P(), P(), P(), P(), P())
    out_specs = P("orbit", "tile", None)
    return jax.shard_map(shards, mesh=mesh, in_specs=in_specs, out_specs=out_specs, check_vma=False)
```

profile of v0, /device:TPU:0, one launch (start us, length us, event | category | flops | bytes accessed | tf_op | source)
XLA Modules:
  0.0 110.7 jit_solution(1591019399376523910)
XLA Ops:
  0.0 2.6 %copy.76 = bf16[4,64,1280]{2,0,1:T(4,128)(2,1)} copy(bf16[4,64,1280]{2,1,0:T(8,128)(2,1)} %param.7) | data formatting | bytes 1310720 | tf_op args[0]
  2.6 0.3 fusion.10
  2.9 5.2 %all-to-all-start = ((bf16[4,64,1280]{2,0,1:T(4,128)(2,1)}), bf16[4,64,1280]{2,0,1:T(4,128)(2,1)}, u32[]{:S(2)}, u32[]{:S(2)}) async-start(bf16[4,64,1280]{2,0,1:T(4,128)(2,1)} %copy.76), calls=%async_computation | async-start | bytes 1310720 | tf_op jit(solution)/shard_map/all_to_all | solution.py:108
  8.1 12.4 %psum.7 = f32[4]{0:T(128)S(1)} all-reduce(f32[4]{0:T(128)S(1)} %fusion.10), channel_id=1, replica_groups=mesh['orbit'=8,'tile'=4] {'tile'}, use_global_device_ids=true, to_apply=%region_3.4 | all-reduce | flops 4 | bytes 32 | tf_op jit(solution)/shard_map/psum | solution.py:103
  20.5 1.3 %fusion.11 = bf16[4,64,1280]{2,1,0:T(8,128)(2,1)S(1)} fusion(bf16[4,64,1280]{2,1,0:T(8,128)(2,1)} %param.8, f32[4]{0:T(128)S(1)} %add_rsqrt_fusion), kind=kLoop, calls=%fused_computation.23 | loop fusion | flops 983040 | bytes 1310736 | tf_op jit(solution)/shard_map/convert_element_type | solution.py:105
  21.8 1.4 %copy.82 = bf16[4,64,1280]{2,0,1:T(4,128)(2,1)} copy(bf16[4,64,1280]{2,1,0:T(8,128)(2,1)S(1)} %fusion.11) | data formatting | bytes 1310720 | tf_op jit(solution)/shard_map/convert_element_type | solution.py:105
  23.2 4.2 %all-to-all-start.1 = ((bf16[4,64,1280]{2,0,1:T(4,128)(2,1)}), bf16[4,64,1280]{2,0,1:T(4,128)(2,1)}, u32[]{:S(2)}, u32[]{:S(2)}) async-start(bf16[4,64,1280]{2,0,1:T(4,128)(2,1)} %copy.82), calls=%async_computation.1 | async-start | bytes 1310720 | tf_op jit(solution)/shard_map/all_to_all | solution.py:109
  27.4 1.2 %convert_bitcast_fusion = f32[8,4,8,1280]{3,2,0,1:T(8,128)S(1)} fusion(bf16[4,64,1280]{2,0,1:T(4,128)(2,1)} %all-to-all-done), kind=kLoop, calls=%fused_computation.40 | loop fusion | flops 327680 | bytes 1966080 | tf_op jit(solution)/shard_map/convert_element_type | solution.py:11
  28.6 0.1 copy.78
  28.7 0.0 copy-start.14
  28.7 0.2 fusion.37
  28.9 0.5 copy-done.14
  29.4 0.4 fusion.17
  29.9 0.8 copy-done.12
  30.7 0.9 copy-done.3
  31.6 1.9 %convolution_convert_fusion.2 = bf16[256,1280]{1,0:T(8,128)(2,1)} fusion(bf16[256,1280]{1,0:T(8,128)(2,1)S(1)} %fusion.17, bf16[1280,1280]{1,0:T(8,128)(2,1)S(1)} %copy-done.3), kind=kOutput, calls=%fused_computation.13 | convolution fusion | flops 839188480 | bytes 4587520 | tf_op jit(solution)/shard_map/dot_general | solution.py:35
  33.5 3.0 %reshape_reshape.18 = bf16[32,8,20,64]{3,2,1,0:T(8,128)(2,1)} reshape(bf16[256,1280]{1,0:T(8,128)(2,1)} %convolution_convert_fusion.2) | data formatting | bytes 1310720 | tf_op jit(solution)/shard_map/reshape;reshape | solution.py:64
  36.4 2.9 %convolution_convert_fusion.1 = bf16[256,1280]{1,0:T(8,128)(2,1)} fusion(bf16[256,1280]{1,0:T(8,128)(2,1)} %copy-done.12, bf16[1280,1280]{1,0:T(8,128)(2,1)S(1)} %copy-done), kind=kOutput, calls=%fused_computation.12 | convolution fusion | flops 839188480 | bytes 4587520 | tf_op jit(solution)/shard_map/dot_general | solution.py:35
  39.4 3.0 %reshape_reshape.19 = bf16[32,8,20,64]{3,2,1,0:T(8,128)(2,1)} reshape(bf16[256,1280]{1,0:T(8,128)(2,1)} %convolution_convert_fusion.1) | data formatting | bytes 1310720 | tf_op jit(solution)/shard_map/reshape;reshape | solution.py:63
  42.3 3.6 %fusion.24 = f32[8,20,32,32]{2,3,1,0:T(8,128)S(1)} fusion(bf16[32,8,20,64]{3,2,1,0:T(8,128)(2,1)} %reshape_reshape.18, bf16[32,8,20,64]{3,2,1,0:T(8,128)(2,1)} %reshape_reshape.19), kind=kOutput, calls=%fused_computation.46 | convolution fusion | flops 20971520 | bytes 1966080 | tf_op jit(solution)/shard_map/fshd,gshd->shfg/dot_general | solution.py:68
  46.0 2.3 %fusion.39 = (f32[8,20,32]{2,1,0:T(8,128)S(1)}, f32[8,20,32,32]{2,3,1,0:T(8,128)}) fusion(f32[8,20,32,32]{2,3,1,0:T(8,128)S(1)} %fusion.24), kind=kOutput, calls=%fused_computation.67 | output fusion | flops 655391 | bytes 1331200 | tf_op jit(solution)/shard_map/sub | solution.py:72
  48.3 2.0 %copy.122 = bf16[4,8,8,1280]{3,2,0,1:T(8,128)(2,1)} copy(bf16[4,8,8,1280]{3,0,2,1:T(4,128)(2,1)} %bitcast.7) | data formatting | bytes 1310720 | tf_op jit(solution)/shard_map/all_to_all | solution.py:109
  50.3 3.0 %reshape.30 = bf16[32,8,20,64]{3,2,1,0:T(8,128)(2,1)} reshape(bf16[8,4,8,1280]{3,2,1,0:T(8,128)(2,1)} %bitcast.84) | data formatting | bytes 1310720 | tf_op jit(solution)/shard_map/reshape | solution.py:66
  53.2 4.1 %convolution_convert_fusion = bf16[256,1280]{1,0:T(8,128)(2,1)} fusion(bf16[256,1280]{1,0:T(8,128)(2,1)} %copy-done.12, bf16[1280,1280]{1,0:T(8,128)(2,1)} %param.11), kind=kOutput, calls=%fused_computation.11 | convolution fusion | flops 839188480 | bytes 4587520 | tf_op jit(solution)/shard_map/dot_general | solution.py:35
  57.3 3.0 %reshape_reshape.20 = bf16[32,8,20,64]{3,2,1,0:T(8,128)(2,1)} reshape(bf16[256,1280]{1,0:T(8,128)(2,1)} %convolution_convert_fusion) | data formatting | bytes 1310720 | tf_op jit(solution)/shard_map/reshape;reshape | solution.py:65
  60.3 3.4 %fusion.7 = bf16[32,8,20,64]{3,0,2,1:T(8,128)(2,1)S(1)} fusion(bf16[32,8,20,64]{3,2,1,0:T(8,128)(2,1)} %reshape.30, f32[8,20,32,32]{2,3,1,0:T(8,128)} %get-tuple-element.17, f32[8,20,32]{2,1,0:T(8,128)S(1)} %get-tuple-element.16), kind=kOutput, calls=%fused_computation.19 | convolution fusion | flops 21626880 | bytes 1986560 | tf_op jit(solution)/shard_map/shfg,fshd->gshd/dot_general | solution.py:77
  63.7 0.1 copy-done.10
  63.8 0.5 copy-done.11
  64.3 2.1 %fusion.1 = f32[32,8,20]{0,2,1:T(8,128)S(1)} fusion(bf16[32,8,20,64]{3,2,1,0:T(8,128)(2,1)S(1)} %copy-done.11, bf16[32,8,20,64]{3,2,1,0:T(8,128)(2,1)S(1)} %copy-done.10, f32[8,20,32,32]{2,3,1,0:T(8,128)S(1)} %copy-done.6, f32[8,20,32]{2,1,0:T(8,128)S(1)} %get-tuple-element.16), kind=kOutput, calls=%fused_computation.4 | convolution fusion | flops 22277120 | bytes 2007040 | tf_op jit(solution)/shard_map/shfg,gshd->fshd/dot_general | solution.py:75
  66.4 2.1 %multiply_convert_fusion.2 = bf16[8,20,32,32]{2,3,1,0:T(8,128)(2,1)S(1)} fusion(f32[8,20,32]{2,1,0:T(8,128)S(1)} %bitcast.85, bf16[32,8,20,64]{3,2,1,0:T(8,128)(2,1)S(1)} %copy-done.11, f32[8,20,32,32]{2,3,1,0:T(8,128)S(1)} %copy-done.6, f32[8,20,32]{2,1,0:T(8,128)S(1)} %get-tuple-element.16, bf16[32,8,20,64]{3,2,1,0:T(8,128)(2,1)S(1)} %copy-done.10), kind=kOutput, calls=%fused_computation.7 | convolution fusion | flops 21626880 | bytes 2334720 | tf_op jit(solution)/shard_map/fshd,gshd->shfg/dot_general | solution.py:80
  68.5 0.0 copy-start.1
  68.5 2.0 %fusion.9 = bf16[32,8,20,64]{3,0,2,1:T(8,128)(2,1)} fusion(bf16[8,20,32,32]{2,3,1,0:T(8,128)(2,1)S(1)} %multiply_convert_fusion.2, bf16[32,8,20,64]{3,2,1,0:T(8,128)(2,1)S(1)} %copy-done.2), kind=kOutput, calls=%fused_computation.21 | convolution fusion | flops 21626880 | bytes 1638400 | tf_op jit(solution)/shard_map/shfg,fshd->gshd/dot_general | solution.py:88
  70.5 2.3 %fusion.8 = bf16[32,8,20,64]{3,0,2,1:T(8,128)(2,1)} fusion(bf16[8,20,32,32]{2,3,1,0:T(8,128)(2,1)S(1)} %multiply_convert_fusion.2, bf16[32,8,20,64]{3,2,1,0:T(8,128)(2,1)S(1)} %copy-done.1), kind=kOutput, calls=%fused_computation.20 | convolution fusion | flops 21626880 | bytes 1638400 | tf_op jit(solution)/shard_map/shfg,gshd->fshd/dot_general | solution.py:84
  72.8 1.7 %copy.96 = bf16[32,8,20,64]{3,2,1,0:T(8,128)(2,1)} copy(bf16[32,8,20,64]{3,0,2,1:T(8,128)(2,1)S(1)} %fusion.7) | data formatting | bytes 1310720 | tf_op jit(solution)/shard_map/convert_element_type | solution.py:79
  74.5 2.7 %reshape_reshape.23 = bf16[256,1280]{1,0:T(8,128)(2,1)} reshape(bf16[32,8,20,64]{3,2,1,0:T(8,128)(2,1)} %copy.96) | data formatting | bytes 1310720 | tf_op jit(solution)/shard_map/reshape;reshape | solution.py:53
  77.3 3.0 %copy.94 = bf16[32,8,20,64]{3,2,1,0:T(8,128)(2,1)} copy(bf16[32,8,20,64]{3,0,2,1:T(8,128)(2,1)} %fusion.9) | data formatting | bytes 1310720 | tf_op jit(solution)/shard_map/convert_element_type | solution.py:90
  80.3 2.8 %reshape_reshape.22 = bf16[256,1280]{1,0:T(8,128)(2,1)} reshape(bf16[32,8,20,64]{3,2,1,0:T(8,128)(2,1)} %copy.94) | data formatting | bytes 1310720 | tf_op jit(solution)/shard_map/reshape;reshape | solution.py:50
  83.0 3.0 %copy.92 = bf16[32,8,20,64]{3,2,1,0:T(8,128)(2,1)} copy(bf16[32,8,20,64]{3,0,2,1:T(8,128)(2,1)} %fusion.8) | data formatting | bytes 1310720 | tf_op jit(solution)/shard_map/convert_element_type | solution.py:86
  86.1 2.7 %reshape_reshape.21 = bf16[256,1280]{1,0:T(8,128)(2,1)} reshape(bf16[32,8,20,64]{3,2,1,0:T(8,128)(2,1)} %copy.92) | data formatting | bytes 1310720 | tf_op jit(solution)/shard_map/reshape;reshape | solution.py:47
  88.8 2.3 %fusion.40 = f32[256,1280]{1,0:T(8,128)S(1)} fusion(bf16[256,1280]{1,0:T(8,128)(2,1)} %reshape_reshape.21, bf16[1280,1280]{1,0:T(8,128)(2,1)S(1)} %copy-done), kind=kOutput, calls=%fused_computation.68 | convolution fusion | flops 838860800 | bytes 5242880 | tf_op jit(solution)/shard_map/dot_general | solution.py:46
  91.1 1.0 convolution_add_fusion.1
  92.2 0.9 copy-done.5
  93.1 0.1 copy-done.8
  93.2 1.0 fusion.3
  94.3 0.2 slice_bitcast_fusion
  94.4 0.3 fusion.22
  94.8 15.0 %all_to_all.42 = bf16[32,8,1280]{2,1,0:T(8,128)(2,1)S(1)} all-to-all(bf16[32,8,1280]{2,1,0:T(8,128)(2,1)S(1)} %fusion.22), channel_id=1, replica_groups=mesh['orbit'=8,'tile'=4] {'orbit'}, dimensions={0} | all-to-all | bytes 1310720 | tf_op jit(solution)/shard_map/all_to_all | solution.py:116
  109.8 0.9 copy.121
  (27 shorter events, 0.1 us)
Async XLA Ops:
  0.0 36.4 %copy-start = (bf16[1280,1280]{1,0:T(8,128)(2,1)S(1)}, bf16[1280,1280]{1,0:T(8,128)(2,1)}, u32[]{:S(2)}) copy-start(bf16[1280,1280]{1,0:T(8,128)(2,1)} %param.9) | copy-start | bytes 9830404
  0.0 2.6 %copy-start.7 = (bf16[4,64,1280]{2,1,0:T(8,128)(2,1)S(1)}, bf16[4,64,1280]{2,1,0:T(8,128)(2,1)}, u32[]{:S(2)}) copy-start(bf16[4,64,1280]{2,1,0:T(8,128)(2,1)} %param.8) | copy-start | bytes 1966084
  2.9 20.3 %all-to-all-start = ((bf16[4,64,1280]{2,0,1:T(4,128)(2,1)}), bf16[4,64,1280]{2,0,1:T(4,128)(2,1)}, u32[]{:S(2)}, u32[]{:S(2)}) async-start(bf16[4,64,1280]{2,0,1:T(4,128)(2,1)} %copy.76), calls=%async_computation | async-start | bytes 1310720 | tf_op jit(solution)/shard_map/all_to_all | solution.py:108
  20.5 2.6 %copy-start.13 = (f32[3,1280]{1,0:T(4,128)S(1)}, f32[3,1280]{1,0:T(4,128)}, u32[]{:S(2)}) copy-start(f32[3,1280]{1,0:T(4,128)} %param.12) | copy-start | bytes 46084
  23.2 25.1 %all-to-all-start.1 = ((bf16[4,64,1280]{2,0,1:T(4,128)(2,1)}), bf16[4,64,1280]{2,0,1:T(4,128)(2,1)}, u32[]{:S(2)}, u32[]{:S(2)}) async-start(bf16[4,64,1280]{2,0,1:T(4,128)(2,1)} %copy.82), calls=%async_computation.1 | async-start | bytes 1310720 | tf_op jit(solution)/shard_map/all_to_all | solution.py:109
  28.7 0.7 copy-start.14
  29.4 2.2 %copy-start.3 = (bf16[1280,1280]{1,0:T(8,128)(2,1)S(1)}, bf16[1280,1280]{1,0:T(8,128)(2,1)}, u32[]{:S(2)}) copy-start(bf16[1280,1280]{1,0:T(8,128)(2,1)} %param.10) | copy-start | bytes 9830404
  29.8 0.8 copy-start.12
  60.3 3.4 %copy-start.6 = (f32[8,20,32,32]{2,3,1,0:T(8,128)S(1)}, f32[8,20,32,32]{2,3,1,0:T(8,128)}, u32[]{:S(2)}) copy-start(f32[8,20,32,32]{2,3,1,0:T(8,128)} %get-tuple-element.17) | copy-start | bytes 1966084
  60.3 3.5 %copy-start.10 = (bf16[32,8,20,64]{3,2,1,0:T(8,128)(2,1)S(1)}, bf16[32,8,20,64]{3,2,1,0:T(8,128)(2,1)}, u32[]{:S(2)}) copy-start(bf16[32,8,20,64]{3,2,1,0:T(8,128)(2,1)} %reshape.30) | copy-start | bytes 1966084
  60.3 3.9 %copy-start.11 = (bf16[32,8,20,64]{3,2,1,0:T(8,128)(2,1)S(1)}, bf16[32,8,20,64]{3,2,1,0:T(8,128)(2,1)}, u32[]{:S(2)}) copy-start(bf16[32,8,20,64]{3,2,1,0:T(8,128)(2,1)} %reshape_reshape.20) | copy-start | bytes 1966084
  66.4 2.1 %copy-start.2 = (bf16[32,8,20,64]{3,2,1,0:T(8,128)(2,1)S(1)}, bf16[32,8,20,64]{3,2,1,0:T(8,128)(2,1)}, u32[]{:S(2)}) copy-start(bf16[32,8,20,64]{3,2,1,0:T(8,128)(2,1)} %reshape_reshape.19) | copy-start | bytes 1966084
  68.5 2.1 %copy-start.1 = (bf16[32,8,20,64]{3,2,1,0:T(8,128)(2,1)S(1)}, bf16[32,8,20,64]{3,2,1,0:T(8,128)(2,1)}, u32[]{:S(2)}) copy-start(bf16[32,8,20,64]{3,2,1,0:T(8,128)(2,1)} %reshape_reshape.18) | copy-start | bytes 1966084
  88.8 2.3 %copy-start.4 = (bf16[1280,1280]{1,0:T(8,128)(2,1)S(1)}, bf16[1280,1280]{1,0:T(8,128)(2,1)}, u32[]{:S(2)}) copy-start(bf16[1280,1280]{1,0:T(8,128)(2,1)} %param.10) | copy-start | bytes 9830404
  88.8 2.3 %copy-start.9 = (bf16[256,1280]{1,0:T(8,128)(2,1)S(1)}, bf16[256,1280]{1,0:T(8,128)(2,1)}, u32[]{:S(2)}) copy-start(bf16[256,1280]{1,0:T(8,128)(2,1)} %reshape_reshape.22) | copy-start | bytes 1966084
  91.1 1.9 %copy-start.5 = (bf16[1280,1280]{1,0:T(8,128)(2,1)S(1)}, bf16[1280,1280]{1,0:T(8,128)(2,1)}, u32[]{:S(2)}) copy-start(bf16[1280,1280]{1,0:T(8,128)(2,1)} %param.11) | copy-start | bytes 9830404
  91.1 2.1 %copy-start.8 = (bf16[256,1280]{1,0:T(8,128)(2,1)S(1)}, bf16[256,1280]{1,0:T(8,128)(2,1)}, u32[]{:S(2)}) copy-start(bf16[256,1280]{1,0:T(8,128)(2,1)} %reshape_reshape.23) | copy-start | bytes 1966084
where the time goes:
time: 111 us
  local copies, waits for them, and re-layouts  39 us (35%)
  matrix products  28.8 us (26%)
  blocking collectives  27.5 us (25%)
  starting transfers between devices  9.41 us (8%)
  other arithmetic  5.8 us (5%)
    all_to_all x1, blocking collectives, shards(): lax.all_to_all(grad_input, 'orbit', split_axis=0, concat_axis=1, tiled=True)  15 us
    psum x1, blocking collectives, shards(): energy = lax.psum(jnp.sum(grad_f * grad_f, axis=(1, 2)), 'tile')  12.4 us
    dot_general x3, matrix products, project_all(): jnp.dot(flat_rows, weight, preferred_element_type=jnp.float32)  8.88 us
    unnamed x31, local copies, waits for them, and re-layouts  6.42 us
    all_to_all x1, starting transfers between devices, shards(): lax.all_to_all(tokens, 'orbit', split_axis=1, concat_axis=0, tiled=True)  5.2 us
    all_to_all x1, starting transfers between devices, shards(): lax.all_to_all(grad_out, 'orbit', split_axis=1, concat_axis=0, tiled=True)  4.21 us
    dot_general x1, matrix products, attention_grads(): jnp.einsum('fshd,gshd->shfg', q_heads, k_heads, preferred_element_type=jn...  3.62 us
    dot_general x1, matrix products, attention_grads(): jnp.einsum('shfg,fshd->gshd', prob_low, g_heads, preferred_element_type=j...  3.35 us
  transfers between devices with their start and end apart: 2, of which 0 were waited for; matrix products, arithmetic and copies ran while one was open for 19% of the time, Pallas kernels for 0%

commit v1 on v0

--- a/solution.py
+++ b/solution.py
@@ -100,7 +100,7 @@
     frame_rows, tile_rows, channels = tokens.shape
     spatial_all = tile_rows * lax.axis_size("tile")
     grad_f = cotangent.astype(jnp.float32)
-    energy = lax.psum(jnp.sum(grad_f * grad_f, axis=(1, 2)), "tile")
+    energy = jnp.sum(lax.all_gather(jnp.sum(grad_f * grad_f, axis=(1, 2)), "tile"), axis=0)
     factor = lax.rsqrt(energy / (spatial_all * channels) + 1e-06)
     grad_out = (grad_f * factor[:, None, None]).astype(jnp.bfloat16)
     weights = (w_query, w_key, w_value)

time: 111 us -> 114 us (1.027)
    psum x1 -> x0, blocking collectives: 12.4 us -> none  [shards(): energy = lax.psum(jnp.sum(grad_f * grad_f, axis=(1, 2)), 'tile')]
    unnamed x0 -> x1, blocking collectives: none -> 12.4 us
    unnamed x31 -> x34, local copies, waits for them, and re-layouts: 6.42 us -> 7.25 us
  transfers between devices with their start and end apart: 2 -> 2, of which waited for: 0 -> 0; matrix products, arithmetic and copies ran while one was open for 19% -> 21% of each run, Pallas kernels for 0% -> 0%
where the time goes in v1:
time: 114 us; the launch traced here: 113 us
  local copies, waits for them, and re-layouts  39.9 us (35%)
  matrix products  28.7 us (25%)
  blocking collectives  27.4 us (24%)
  starting transfers between devices  9.55 us (8%)
  other arithmetic  6.91 us (6%)
    all_to_all x1, blocking collectives, shards(): lax.all_to_all(grad_input, 'orbit', split_axis=0, concat_axis=1, tiled=True)  15 us
    unnamed x1, blocking collectives  12.4 us
    dot_general x3, matrix products, project_all(): jnp.dot(flat_rows, weight, preferred_element_type=jnp.float32)  8.87 us
    unnamed x34, local copies, waits for them, and re-layouts  7.25 us
    all_to_all x1, starting transfers between devices, shards(): lax.all_to_all(tokens, 'orbit', split_axis=1, concat_axis=0, tiled=True)  5.33 us
    all_to_all x1, starting transfers between devices, shards(): lax.all_to_all(grad_out, 'orbit', split_axis=1, concat_axis=0, tiled=True)  4.22 us
    dot_general x1, matrix products, attention_grads(): jnp.einsum('fshd,gshd->shfg', q_heads, k_heads, preferred_element_type=jn...  3.62 us
    dot_general x1, matrix products, attention_grads(): jnp.einsum('shfg,fshd->gshd', prob_low, g_heads, preferred_element_type=j...  3.35 us
  transfers between devices with their start and end apart: 2, of which 0 were waited for; matrix products, arithmetic and copies ran while one was open for 21% of the time, Pallas kernels for 0%

profile of v1, /device:TPU:0, one launch (start us, length us, event | category | flops | bytes accessed | tf_op | source)
XLA Modules:
  0.0 113.4 jit_solution(10136315706134964401)
XLA Ops:
  0.0 2.6 %copy.76 = bf16[4,64,1280]{2,0,1:T(4,128)(2,1)} copy(bf16[4,64,1280]{2,1,0:T(8,128)(2,1)} %param.7) | data formatting | bytes 1310720 | tf_op args[0]
  2.6 5.3 %all-to-all-start = ((bf16[4,64,1280]{2,0,1:T(4,128)(2,1)}), bf16[4,64,1280]{2,0,1:T(4,128)(2,1)}, u32[]{:S(2)}, u32[]{:S(2)}) async-start(bf16[4,64,1280]{2,0,1:T(4,128)(2,1)} %copy.76), calls=%async_computation | async-start | bytes 1310720 | tf_op jit(solution)/shard_map/all_to_all | solution.py:108
  7.9 1.3 %fusion.10 = f32[4]{0:T(128)S(1)} fusion(bf16[4,64,1280]{2,1,0:T(8,128)(2,1)} %param.8), kind=kLoop, calls=%fused_computation.22 | loop fusion | flops 983036 | bytes 655376 | tf_op jit(solution)/shard_map/reduce_sum | solution.py:103
  9.3 0.6 dynamic-slice
  10.5 0.2 dynamic-update-slice
  10.7 12.4 %all-reduce = f32[16]{0:T(128)S(1)} all-reduce(f32[16]{0:T(128)S(1)} %dynamic-update-slice), channel_id=2, replica_groups=mesh['orbit'=8,'tile'=4] {'tile'}, use_global_device_ids=true, to_apply=%add | all-reduce | flops 16 | bytes 128
  23.2 0.1 reshape.39
  23.3 1.3 %fusion.11 = bf16[4,64,1280]{2,1,0:T(8,128)(2,1)S(1)} fusion(bf16[4,64,1280]{2,1,0:T(8,128)(2,1)} %param.8, f32[4]{0:T(128)S(1)} %add_rsqrt_fusion), kind=kLoop, calls=%fused_computation.23 | loop fusion | flops 983040 | bytes 1310736 | tf_op jit(solution)/shard_map/convert_element_type | solution.py:105
  24.6 1.4 %copy.82 = bf16[4,64,1280]{2,0,1:T(4,128)(2,1)} copy(bf16[4,64,1280]{2,1,0:T(8,128)(2,1)S(1)} %fusion.11) | data formatting | bytes 1310720 | tf_op jit(solution)/shard_map/convert_element_type | solution.py:105
  26.0 4.2 %all-to-all-start.1 = ((bf16[4,64,1280]{2,0,1:T(4,128)(2,1)}), bf16[4,64,1280]{2,0,1:T(4,128)(2,1)}, u32[]{:S(2)}, u32[]{:S(2)}) async-start(bf16[4,64,1280]{2,0,1:T(4,128)(2,1)} %copy.82), calls=%async_computation.1 | async-start | bytes 1310720 | tf_op jit(solution)/shard_map/all_to_all | solution.py:109
  30.2 1.2 %convert_bitcast_fusion = f32[8,4,8,1280]{3,2,0,1:T(8,128)S(1)} fusion(bf16[4,64,1280]{2,0,1:T(4,128)(2,1)} %all-to-all-done), kind=kLoop, calls=%fused_computation.40 | loop fusion | flops 327680 | bytes 1966080 | tf_op jit(solution)/shard_map/convert_element_type | solution.py:11
  31.4 0.1 copy.78
  31.5 0.2 fusion.37
  31.7 0.5 copy-done.13
  32.2 0.4 fusion.17
  32.6 0.8 copy-done.11
  33.5 0.9 copy-done.3
  34.4 1.9 %convolution_convert_fusion.2 = bf16[256,1280]{1,0:T(8,128)(2,1)} fusion(bf16[256,1280]{1,0:T(8,128)(2,1)S(1)} %fusion.17, bf16[1280,1280]{1,0:T(8,128)(2,1)S(1)} %copy-done.3), kind=kOutput, calls=%fused_computation.13 | convolution fusion | flops 839188480 | bytes 4587520 | tf_op jit(solution)/shard_map/dot_general | solution.py:35
  36.2 3.0 %reshape_reshape.18 = bf16[32,8,20,64]{3,2,1,0:T(8,128)(2,1)} reshape(bf16[256,1280]{1,0:T(8,128)(2,1)} %convolution_convert_fusion.2) | data formatting | bytes 1310720 | tf_op jit(solution)/shard_map/reshape;reshape | solution.py:64
  39.2 2.9 %convolution_convert_fusion.1 = bf16[256,1280]{1,0:T(8,128)(2,1)} fusion(bf16[256,1280]{1,0:T(8,128)(2,1)} %copy-done.11, bf16[1280,1280]{1,0:T(8,128)(2,1)S(1)} %copy-done), kind=kOutput, calls=%fused_computation.12 | convolution fusion | flops 839188480 | bytes 4587520 | tf_op jit(solution)/shard_map/dot_general | solution.py:35
  42.2 3.0 %reshape_reshape.19 = bf16[32,8,20,64]{3,2,1,0:T(8,128)(2,1)} reshape(bf16[256,1280]{1,0:T(8,128)(2,1)} %convolution_convert_fusion.1) | data formatting | bytes 1310720 | tf_op jit(solution)/shard_map/reshape;reshape | solution.py:63
  45.1 3.6 %fusion.24 = f32[8,20,32,32]{2,3,1,0:T(8,128)S(1)} fusion(bf16[32,8,20,64]{3,2,1,0:T(8,128)(2,1)} %reshape_reshape.18, bf16[32,8,20,64]{3,2,1,0:T(8,128)(2,1)} %reshape_reshape.19), kind=kOutput, calls=%fused_computation.46 | convolution fusion | flops 20971520 | bytes 1966080 | tf_op jit(solution)/shard_map/fshd,gshd->shfg/dot_general | solution.py:68
  48.7 2.3 %fusion.39 = (f32[8,20,32]{2,1,0:T(8,128)S(1)}, f32[8,20,32,32]{2,3,1,0:T(8,128)}) fusion(f32[8,20,32,32]{2,3,1,0:T(8,128)S(1)} %fusion.24), kind=kOutput, calls=%fused_computation.67 | output fusion | flops 655391 | bytes 1331200 | tf_op jit(solution)/shard_map/sub | solution.py:72
  51.1 2.0 %copy.122 = bf16[4,8,8,1280]{3,2,0,1:T(8,128)(2,1)} copy(bf16[4,8,8,1280]{3,0,2,1:T(4,128)(2,1)} %bitcast.8) | data formatting | bytes 1310720 | tf_op jit(solution)/shard_map/all_to_all | solution.py:109
  53.0 3.0 %reshape.34 = bf16[32,8,20,64]{3,2,1,0:T(8,128)(2,1)} reshape(bf16[8,4,8,1280]{3,2,1,0:T(8,128)(2,1)} %bitcast.85) | data formatting | bytes 1310720 | tf_op jit(solution)/shard_map/reshape | solution.py:66
  56.0 4.1 %convolution_convert_fusion = bf16[256,1280]{1,0:T(8,128)(2,1)} fusion(bf16[256,1280]{1,0:T(8,128)(2,1)} %copy-done.11, bf16[1280,1280]{1,0:T(8,128)(2,1)} %param.11), kind=kOutput, calls=%fused_computation.11 | convolution fusion | flops 839188480 | bytes 4587520 | tf_op jit(solution)/shard_map/dot_general | solution.py:35
  60.1 3.0 %reshape_reshape.20 = bf16[32,8,20,64]{3,2,1,0:T(8,128)(2,1)} reshape(bf16[256,1280]{1,0:T(8,128)(2,1)} %convolution_convert_fusion) | data formatting | bytes 1310720 | tf_op jit(solution)/shard_map/reshape;reshape | solution.py:65
  63.1 3.4 %fusion.7 = bf16[32,8,20,64]{3,0,2,1:T(8,128)(2,1)S(1)} fusion(bf16[32,8,20,64]{3,2,1,0:T(8,128)(2,1)} %reshape.34, f32[8,20,32,32]{2,3,1,0:T(8,128)} %get-tuple-element.17, f32[8,20,32]{2,1,0:T(8,128)S(1)} %get-tuple-element.16), kind=kOutput, calls=%fused_computation.19 | convolution fusion | flops 21626880 | bytes 1986560 | tf_op jit(solution)/shard_map/shfg,fshd->gshd/dot_general | solution.py:77
  66.5 0.5 copy-done.10
  67.0 2.1 %fusion.1 = f32[32,8,20]{0,2,1:T(8,128)S(1)} fusion(bf16[32,8,20,64]{3,2,1,0:T(8,128)(2,1)S(1)} %copy-done.10, bf16[32,8,20,64]{3,2,1,0:T(8,128)(2,1)S(1)} %copy-done.9, f32[8,20,32,32]{2,3,1,0:T(8,128)S(1)} %copy-done.6, f32[8,20,32]{2,1,0:T(8,128)S(1)} %get-tuple-element.16), kind=kOutput, calls=%fused_computation.4 | convolution fusion | flops 22277120 | bytes 2007040 | tf_op jit(solution)/shard_map/shfg,gshd->fshd/dot_general | solution.py:75
  69.2 2.1 %multiply_convert_fusion.2 = bf16[8,20,32,32]{2,3,1,0:T(8,128)(2,1)S(1)} fusion(f32[8,20,32]{2,1,0:T(8,128)S(1)} %bitcast.86, bf16[32,8,20,64]{3,2,1,0:T(8,128)(2,1)S(1)} %copy-done.10, f32[8,20,32,32]{2,3,1,0:T(8,128)S(1)} %copy-done.6, f32[8,20,32]{2,1,0:T(8,128)S(1)} %get-tuple-element.16, bf16[32,8,20,64]{3,2,1,0:T(8,128)(2,1)S(1)} %copy-done.9), kind=kOutput, calls=%fused_computation.7 | convolution fusion | flops 21626880 | bytes 2334720 | tf_op jit(solution)/shard_map/fshd,gshd->shfg/dot_general | solution.py:80
  71.2 2.0 %fusion.9 = bf16[32,8,20,64]{3,0,2,1:T(8,128)(2,1)} fusion(bf16[8,20,32,32]{2,3,1,0:T(8,128)(2,1)S(1)} %multiply_convert_fusion.2, bf16[32,8,20,64]{3,2,1,0:T(8,128)(2,1)S(1)} %copy-done.2), kind=kOutput, calls=%fused_computation.21 | convolution fusion | flops 21626880 | bytes 1638400 | tf_op jit(solution)/shard_map/shfg,fshd->gshd/dot_general | solution.py:88
  73.3 2.3 %fusion.8 = bf16[32,8,20,64]{3,0,2,1:T(8,128)(2,1)} fusion(bf16[8,20,32,32]{2,3,1,0:T(8,128)(2,1)S(1)} %multiply_convert_fusion.2, bf16[32,8,20,64]{3,2,1,0:T(8,128)(2,1)S(1)} %copy-done.1), kind=kOutput, calls=%fused_computation.20 | convolution fusion | flops 21626880 | bytes 1638400 | tf_op jit(solution)/shard_map/shfg,gshd->fshd/dot_general | solution.py:84
  75.6 1.7 %copy.96 = bf16[32,8,20,64]{3,2,1,0:T(8,128)(2,1)} copy(bf16[32,8,20,64]{3,0,2,1:T(8,128)(2,1)S(1)} %fusion.7) | data formatting | bytes 1310720 | tf_op jit(solution)/shard_map/convert_element_type | solution.py:79
  77.2 2.7 %reshape_reshape.23 = bf16[256,1280]{1,0:T(8,128)(2,1)} reshape(bf16[32,8,20,64]{3,2,1,0:T(8,128)(2,1)} %copy.96) | data formatting | bytes 1310720 | tf_op jit(solution)/shard_map/reshape;reshape | solution.py:53
  80.0 3.0 %copy.94 = bf16[32,8,20,64]{3,2,1,0:T(8,128)(2,1)} copy(bf16[32,8,20,64]{3,0,2,1:T(8,128)(2,1)} %fusion.9) | data formatting | bytes 1310720 | tf_op jit(solution)/shard_map/convert_element_type | solution.py:90
  83.0 2.8 %reshape_reshape.22 = bf16[256,1280]{1,0:T(8,128)(2,1)} reshape(bf16[32,8,20,64]{3,2,1,0:T(8,128)(2,1)} %copy.94) | data formatting | bytes 1310720 | tf_op jit(solution)/shard_map/reshape;reshape | solution.py:50
  85.8 3.0 %copy.92 = bf16[32,8,20,64]{3,2,1,0:T(8,128)(2,1)} copy(bf16[32,8,20,64]{3,0,2,1:T(8,128)(2,1)} %fusion.8) | data formatting | bytes 1310720 | tf_op jit(solution)/shard_map/convert_element_type | solution.py:86
  88.8 2.7 %reshape_reshape.21 = bf16[256,1280]{1,0:T(8,128)(2,1)} reshape(bf16[32,8,20,64]{3,2,1,0:T(8,128)(2,1)} %copy.92) | data formatting | bytes 1310720 | tf_op jit(solution)/shard_map/reshape;reshape | solution.py:47
  91.5 2.3 %fusion.40 = f32[256,1280]{1,0:T(8,128)S(1)} fusion(bf16[256,1280]{1,0:T(8,128)(2,1)} %reshape_reshape.21, bf16[1280,1280]{1,0:T(8,128)(2,1)S(1)} %copy-done), kind=kOutput, calls=%fused_computation.68 | convolution fusion | flops 838860800 | bytes 5242880 | tf_op jit(solution)/shard_map/dot_general | solution.py:46
  93.9 1.0 convolution_add_fusion.1
  94.9 0.9 copy-done.5
  95.8 0.1 copy-done.7
  95.9 1.0 fusion.3
  97.0 0.2 slice_bitcast_fusion
  97.2 0.3 fusion.22
  97.5 15.0 %all_to_all.42 = bf16[32,8,1280]{2,1,0:T(8,128)(2,1)S(1)} all-to-all(bf16[32,8,1280]{2,1,0:T(8,128)(2,1)S(1)} %fusion.22), channel_id=1, replica_groups=mesh['orbit'=8,'tile'=4] {'orbit'}, dimensions={0} | all-to-all | bytes 1310720 | tf_op jit(solution)/shard_map/all_to_all | solution.py:116
  112.5 0.9 copy.121
  (32 shorter events, 0.2 us)
Async XLA Ops:
  0.0 39.2 %copy-start = (bf16[1280,1280]{1,0:T(8,128)(2,1)S(1)}, bf16[1280,1280]{1,0:T(8,128)(2,1)}, u32[]{:S(2)}) copy-start(bf16[1280,1280]{1,0:T(8,128)(2,1)} %param.9) | copy-start | bytes 9830404
  2.6 6.7 %copy-start.14 = (u32[32]{0:T(128)S(1)}, u32[32]{0:T(128)}, u32[]{:S(2)}) copy-start(u32[32]{0:T(128)} %constant.16) | copy-start | bytes 388
  2.6 23.4 %all-to-all-start = ((bf16[4,64,1280]{2,0,1:T(4,128)(2,1)}), bf16[4,64,1280]{2,0,1:T(4,128)(2,1)}, u32[]{:S(2)}, u32[]{:S(2)}) async-start(bf16[4,64,1280]{2,0,1:T(4,128)(2,1)} %copy.76), calls=%async_computation | async-start | bytes 1310720 | tf_op jit(solution)/shard_map/all_to_all | solution.py:108
  23.3 2.7 %copy-start.12 = (f32[3,1280]{1,0:T(4,128)S(1)}, f32[3,1280]{1,0:T(4,128)}, u32[]{:S(2)}) copy-start(f32[3,1280]{1,0:T(4,128)} %param.12) | copy-start | bytes 46084
  26.0 25.1 %all-to-all-start.1 = ((bf16[4,64,1280]{2,0,1:T(4,128)(2,1)}), bf16[4,64,1280]{2,0,1:T(4,128)(2,1)}, u32[]{:S(2)}, u32[]{:S(2)}) async-start(bf16[4,64,1280]{2,0,1:T(4,128)(2,1)} %copy.82), calls=%async_computation.1 | async-start | bytes 1310720 | tf_op jit(solution)/shard_map/all_to_all | solution.py:109
  31.5 0.7 copy-start.13
  32.2 2.2 %copy-start.3 = (bf16[1280,1280]{1,0:T(8,128)(2,1)S(1)}, bf16[1280,1280]{1,0:T(8,128)(2,1)}, u32[]{:S(2)}) copy-start(bf16[1280,1280]{1,0:T(8,128)(2,1)} %param.10) | copy-start | bytes 9830404
  32.6 0.8 copy-start.11
  63.1 3.4 %copy-start.6 = (f32[8,20,32,32]{2,3,1,0:T(8,128)S(1)}, f32[8,20,32,32]{2,3,1,0:T(8,128)}, u32[]{:S(2)}) copy-start(f32[8,20,32,32]{2,3,1,0:T(8,128)} %get-tuple-element.17) | copy-start | bytes 1966084
  63.1 3.5 %copy-start.9 = (bf16[32,8,20,64]{3,2,1,0:T(8,128)(2,1)S(1)}, bf16[32,8,20,64]{3,2,1,0:T(8,128)(2,1)}, u32[]{:S(2)}) copy-start(bf16[32,8,20,64]{3,2,1,0:T(8,128)(2,1)} %reshape.34) | copy-start | bytes 1966084
  63.1 3.9 %copy-start.10 = (bf16[32,8,20,64]{3,2,1,0:T(8,128)(2,1)S(1)}, bf16[32,8,20,64]{3,2,1,0:T(8,128)(2,1)}, u32[]{:S(2)}) copy-start(bf16[32,8,20,64]{3,2,1,0:T(8,128)(2,1)} %reshape_reshape.20) | copy-start | bytes 1966084
  69.1 2.1 %copy-start.2 = (bf16[32,8,20,64]{3,2,1,0:T(8,128)(2,1)S(1)}, bf16[32,8,20,64]{3,2,1,0:T(8,128)(2,1)}, u32[]{:S(2)}) copy-start(bf16[32,8,20,64]{3,2,1,0:T(8,128)(2,1)} %reshape_reshape.19) | copy-start | bytes 1966084
  71.2 2.0 %copy-start.1 = (bf16[32,8,20,64]{3,2,1,0:T(8,128)(2,1)S(1)}, bf16[32,8,20,64]{3,2,1,0:T(8,128)(2,1)}, u32[]{:S(2)}) copy-start(bf16[32,8,20,64]{3,2,1,0:T(8,128)(2,1)} %reshape_reshape.18) | copy-start | bytes 1966084
  91.5 2.3 %copy-start.4 = (bf16[1280,1280]{1,0:T(8,128)(2,1)S(1)}, bf16[1280,1280]{1,0:T(8,128)(2,1)}, u32[]{:S(2)}) copy-start(bf16[1280,1280]{1,0:T(8,128)(2,1)} %param.10) | copy-start | bytes 9830404
  91.5 2.3 %copy-start.8 = (bf16[256,1280]{1,0:T(8,128)(2,1)S(1)}, bf16[256,1280]{1,0:T(8,128)(2,1)}, u32[]{:S(2)}) copy-start(bf16[256,1280]{1,0:T(8,128)(2,1)} %reshape_reshape.22) | copy-start | bytes 1966084
  93.9 1.9 %copy-start.5 = (bf16[1280,1280]{1,0:T(8,128)(2,1)S(1)}, bf16[1280,1280]{1,0:T(8,128)(2,1)}, u32[]{:S(2)}) copy-start(bf16[1280,1280]{1,0:T(8,128)(2,1)} %param.11) | copy-start | bytes 9830404
  93.9 2.1 %copy-start.7 = (bf16[256,1280]{1,0:T(8,128)(2,1)S(1)}, bf16[256,1280]{1,0:T(8,128)(2,1)}, u32[]{:S(2)}) copy-start(bf16[256,1280]{1,0:T(8,128)(2,1)} %reshape_reshape.23) | copy-start | bytes 1966084
